TPU v7x, 256 devices: a whole 4x4x8 slice. The times are simulated.
256 devices in a mesh: rep: 4 (over y), dev: 64 (over z, x, core).
Axes of the slice: x: 4, y: 4, z: 8, core: 2. Of those that a mesh axis runs over, the one named last changes fastest.
Arguments:
- theta: bfloat16 [24, 2816, 1024], P(None, 'dev'), may hold values from -6 to 6
- deltas: bfloat16 [4, 24, 2816, 1024], P('rep', None, 'dev'), may hold values from -6 to 6
- momentum: float32 [128, 64, 4, 11, 1024], P('dev', None, 'rep'), may hold values from -2 to 2
- basis: bfloat16 [1024, 64], replicated, may hold values from -0.1875 to 0.1875
- slot_matrix: int32 [128], replicated, may hold values from -1 to 23, as said below
Outputs:
- new_theta: bfloat16 [24, 2816, 1024], P(None, 'dev')
Inputs may be any that keep to these rules, and one draw needn't show every extreme that they name: `slot_matrix`: every matrix 0 to 23 stands in exactly one slot; -1 marks an empty slot; some device fills all 2 of its slots.
All inputs are finite; a program needn't handle non-finite values.
Results may differ from a plain program's by a relative error of at most 0.007.
Values may be sent and summed in bfloat16 or wider, within the bound.
A program may use at most 128 MiB of HBM per device.

v0:
```python
import jax
import jax.numpy as jnp
from jax import lax
from jax.sharding import PartitionSpec as P

momentum_rate = 0.9
outer_rate = 0.7


def per_device(theta, deltas, momentum, basis, slot_matrix):
    rep_count = lax.axis_size("rep")
    dev_count = lax.axis_size("dev")
    matrices = theta.shape[0]
    rows = theta.shape[1]
    width = theta.shape[2]
    slots = momentum.shape[0]
    piece = momentum.shape[3]
    rank = basis.shape[1]
    lookup_table = slot_matrix.reshape(dev_count, slots).T
    filled = lookup_table >= 0
    safe_index = jnp.maximum(lookup_table, 0)
    compressed = jnp.einsum(
        "mfd,dk->mfk", deltas[0], basis, preferred_element_type=jnp.float32
    ).astype(jnp.bfloat16)
    outgoing = jnp.take(compressed.reshape(matrices, rows * rank), safe_index, axis=0)
    outgoing = outgoing * filled[:, :, None].astype(jnp.bfloat16)
    incoming = lax.all_to_all(outgoing, "dev", split_axis=1, concat_axis=1, tiled=True)
    terms = incoming.astype(jnp.float32).reshape(slots, dev_count, rep_count, piece * rank)
    summed = lax.psum_scatter(
        terms.astype(jnp.bfloat16), "rep", scatter_dimension=2, tiled=True
    ).astype(jnp.float32)
    averaged = summed.reshape(slots, dev_count * piece, rank) / rep_count
    outer = jnp.einsum(
        "csk,dk->csd", averaged, basis.astype(jnp.float32), precision=lax.Precision.HIGHEST
    )
    moment = momentum.reshape(slots, dev_count * piece, width)
    renewed = momentum_rate * moment + outer
    update = (outer_rate * (outer + momentum_rate * renewed)).astype(jnp.bfloat16)
    paired_match = slot_matrix[None, :] == jnp.arange(matrices, dtype=jnp.int32)[:, None]
    slot_position = jnp.sum(
        jnp.where(paired_match, jnp.arange(slots * dev_count, dtype=jnp.int32)[None, :], 0), axis=1
    )
    ordering = slot_position % slots * dev_count + slot_position // slots
    spread = lax.all_gather(
        update.reshape(slots, dev_count, 1, piece, width), "rep", axis=2, tiled=True
    )
    landed = lax.all_to_all(spread, "dev", split_axis=1, concat_axis=1, tiled=True)
    chosen = jnp.take(landed.reshape(slots * dev_count, rows, width), ordering, axis=0)
    return (theta.astype(jnp.float32) - chosen.astype(jnp.float32)).astype(jnp.bfloat16)


def solution(mesh):
    placed = (
        P(None, "dev", None),
        P("rep", None, "dev", None),
        P("dev", None, "rep", None, None),
        P(),
        P(),
    )
    return jax.shard_map(
        per_device, mesh=mesh, in_specs=placed, out_specs=P(None, "dev", None), check_vma=False
    )
```

profile of v0, /device:TPU:1, one launch (start us, length us, event | category | flops | bytes accessed | tf_op | source)
XLA Modules:
  0.0 535.7 jit_solution(2369431781940186766)
XLA Ops:
  6.5 0.0 copy-start
  6.5 0.0 reduce-scatter.2.cloned.1.call-start
  6.5 0.8 broadcast_maximum_fusion
  7.3 0.7 compare_convert_fusion
  8.0 0.1 max.10
  8.2 0.1 copy.57
  8.2 0.1 reshape.126
  8.3 0.0 copy-done
  8.3 1.6 fusion.2
  10.0 0.2 reshape.120
  10.2 0.1 reshape.123
  10.4 1.0 gather_fusion
  11.4 1.1 fusion.5
  12.5 34.4 %all_to_all.10 = bf16[2,64,2816]{2,0,1:T(2,128)(2,1)S(1)} all-to-all(bf16[2,64,2816]{2,0,1:T(2,128)(2,1)S(1)} %fusion.5), channel_id=1, replica_groups=mesh['rep'=4,'dev'=64] {'dev'}, dimensions={1} | all-to-all | bytes 1441792 | tf_op jit(solution)/shard_map/all_to_all | solution.py:27
  46.9 1.0 reshape.143
  47.8 1.0 copy.60
  48.9 0.0 reduce-scatter.2.cloned.1.call-update
  48.9 0.2 all-gather.2.cloned.1.call-start
  49.1 21.2 %multiply_reduce_fusion = f32[2,64,11,1024]{3,2,1,0:T(8,128)} fusion(f32[2,64,1,11,1024]{4,2,3,1,0:T(1,128)} %param.7), kind=kLoop, calls=%fused_computation.3 | loop fusion | flops 1441792 | bytes 11534336 | tf_op jit(solution)/shard_map/mul | solution.py:37
  70.3 0.0 copy-start.2
  70.3 7.6 %mul.41 = f32[2,704,1024]{2,1,0:T(8,128)} reshape(f32[2,64,11,1024]{3,2,1,0:T(8,128)} %multiply_reduce_fusion) | data formatting | bytes 11534336 | tf_op jit(solution)/shard_map/mul | solution.py:37
  78.0 0.0 reduce-scatter.2.cloned.1.call-done
  78.0 1.0 convert_multiply_fusion
  78.9 0.2 div.29
  79.1 0.0 copy-done.2
  79.1 5.6 %multiply_convert_fusion = bf16[2,704,1024]{2,1,0:T(8,128)(2,1)S(1)} fusion(f32[2,704,1024]{2,1,0:T(8,128)} %mul.41, f32[2,704,64]{2,1,0:T(8,128)S(1)} %div.29, bf16[1024,64]{0,1:T(8,128)(2,1)S(1)} %copy-done.2), kind=kOutput, calls=%fused_computation.2 | convolution fusion | flops 1114505216 | bytes 9142272 | tf_op jit(solution)/shard_map/csk,dk->csd/dot_general | solution.py:33
  84.8 3.0 copy.62
  87.7 2.6 copy.63
  90.3 0.0 all-gather.2.cloned.1.call-update
  90.4 109.3 %all-gather.2.cloned.1.call-done = bf16[2,64,4,11,1024]{4,1,3,0,2:T(8,128)(2,1)} async-done(((bf16[2,64,1,11,1024]{4,1,3,0,2:T(8,128)(2,1)}), bf16[2,64,4,11,1024]{4,1,3,0,2:T(8,128)(2,1)}) %all-gather.2.cloned.1.call-update) | async-done | bytes 11534352 | tf_op jit(solution)/shard_map/all_gather | solution.py:44
  199.6 22.0 %copy.64 = bf16[2,64,4,11,1024]{4,0,3,2,1:T(2,128)(2,1)} copy(bf16[2,64,4,11,1024]{4,1,3,0,2:T(8,128)(2,1)} %all-gather.2.cloned.1.call-done) | data formatting | bytes 23068672 | tf_op jit(solution)/shard_map/all_gather | solution.py:44
  221.6 0.0 copy-start.3
  221.6 11.0 %all-to-all-start.1 = ((bf16[2,64,4,11,1024]{4,0,3,2,1:T(2,128)(2,1)}), bf16[2,64,4,11,1024]{4,0,3,2,1:T(2,128)(2,1)}, u32[]{:S(2)}, u32[]{:S(2)}) async-start(bf16[2,64,4,11,1024]{4,0,3,2,1:T(2,128)(2,1)} %copy.64), calls=%async_computation.2 | async-start | bytes 23068672 | tf_op jit(solution)/shard_map/all_to_all | solution.py:47
  232.6 0.0 copy-done.3
  232.6 0.1 select_reduce_fusion
  232.8 249.7 %all-to-all-done.1 = bf16[2,64,4,11,1024]{4,0,3,2,1:T(2,128)(2,1)} async-done(((bf16[2,64,4,11,1024]{4,0,3,2,1:T(2,128)(2,1)}), bf16[2,64,4,11,1024]{4,0,3,2,1:T(2,128)(2,1)}, u32[]{:S(2)}, u32[]{:S(2)}) %all-to-all-start.1) | async-done | bytes 11534368 | tf_op jit(solution)/shard_map/all_to_all | solution.py:47
  482.5 12.0 %copy.65 = bf16[2,64,4,11,1024]{4,1,0,3,2:T(8,128)(2,1)S(1)} copy(bf16[2,64,4,11,1024]{4,0,3,2,1:T(2,128)(2,1)} %all-to-all-done.1) | data formatting | bytes 23068672 | tf_op jit(solution)/shard_map/all_to_all | solution.py:47
  494.5 22.1 %copy.66 = bf16[128,44,1024]{2,1,0:T(8,128)(2,1)} copy(bf16[128,44,1024]{2,0,1:T(8,128)(2,1)S(1)} %bitcast.40) | data formatting | bytes 23068672 | tf_op jit(solution)/shard_map/reshape | solution.py:48
  516.6 0.0 copy-start.1
  516.6 6.9 %gather_fusion.1 = bf16[24,44,1024]{2,1,0:T(8,128)(2,1)} fusion(bf16[128,44,1024]{2,1,0:T(8,128)(2,1)} %copy.66, s32[1024]{0:T(1024)S(1)} %pad_clamp_fusion), kind=kCustom, calls=%fused_computation.1 | custom fusion | bytes 4325472 | tf_op jit(solution)/shard_map/jit(_take)/gather | solution.py:48
  523.5 5.4 subtract_convert_fusion
  528.9 0.0 copy-done.1
  (6 shorter events, 0.1 us)
Async XLA Ops:
  6.5 1.8 copy-start
  6.5 71.4 %reduce-scatter.2.cloned.1.call-start = ((), (), s32[]{:S(2)}) async-start(), calls=%async_computation.3 | async-start | bytes 983040 | tf_op jit(solution)/shard_map/reduce_scatter | solution.py:29
  48.9 150.8 %all-gather.2.cloned.1.call-start = ((), (), s32[]{:S(2)}) async-start(), calls=%async_computation.4 | async-start | bytes 14417920 | tf_op jit(solution)/shard_map/all_gather | solution.py:44
  70.3 8.8 %copy-start.2 = (bf16[1024,64]{0,1:T(8,128)(2,1)S(1)}, bf16[1024,64]{0,1:T(8,128)(2,1)}, u32[]{:S(2)}) copy-start(bf16[1024,64]{0,1:T(8,128)(2,1)} %param.8) | copy-start | bytes 393220
  221.6 11.0 %copy-start.3 = (s32[128]{0:T(128)S(1)}, s32[128]{0:T(128)}, u32[]{:S(2)}) copy-start(s32[128]{0:T(128)} %param.9) | copy-start | bytes 1540
  221.6 260.9 %all-to-all-start.1 = ((bf16[2,64,4,11,1024]{4,0,3,2,1:T(2,128)(2,1)}), bf16[2,64,4,11,1024]{4,0,3,2,1:T(2,128)(2,1)}, u32[]{:S(2)}, u32[]{:S(2)}) async-start(bf16[2,64,4,11,1024]{4,0,3,2,1:T(2,128)(2,1)} %copy.64), calls=%async_computation.2 | async-start | bytes 23068672 | tf_op jit(solution)/shard_map/all_to_all | solution.py:47
  516.6 12.3 %copy-start.1 = (bf16[1,24,44,1024]{3,1,2,0:T(8,128)(2,1)S(1)}, bf16[1,24,44,1024]{3,1,2,0:T(8,128)(2,1)}, u32[]{:S(2)}) copy-start(bf16[1,24,44,1024]{3,1,2,0:T(8,128)(2,1)} %param.6) | copy-start | bytes 6488068
Sparse Core Ops, SparseCore 0:
  49.0 20.7 reduce-scatter.1
  90.5 109.1 all-gather.1
where the time goes:
time: 541 us; the launch traced here: 536 us
  waiting for transfers between devices  359 us (66%)
  local copies, waits for them, and re-layouts  80.1 us (15%)
  blocking collectives  34.4 us (6%)
  other arithmetic  30.2 us (6%)
  between operations  13.5 us (2%)
  starting transfers between devices  11.2 us (2%)
  matrix products  7.27 us (1%)
    all_to_all x1, waiting for transfers between devices, per_device(): lax.all_to_all(spread, 'dev', split_axis=1, concat_axis=1, tiled=True)  250 us
    all_gather x1, waiting for transfers between devices, per_device(): lax.all_gather(update.reshape(slots, dev_count, 1, piece, width), 'rep',...  109 us
    all_to_all x1, blocking collectives, per_device(): lax.all_to_all(outgoing, 'dev', split_axis=1, concat_axis=1, tiled=True)  34.4 us
    reshape x1, local copies, waits for them, and re-layouts, per_device(): landed.reshape(slots * dev_count, rows, width)  22.1 us
    all_gather x1, local copies, waits for them, and re-layouts, per_device(): lax.all_gather(update.reshape(slots, dev_count, 1, piece, width), 'rep',...  22 us
    mul x1, other arithmetic, per_device(): renewed = momentum_rate * moment + outer  21.2 us
    all_to_all x1, local copies, waits for them, and re-layouts, per_device(): lax.all_to_all(spread, 'dev', split_axis=1, concat_axis=1, tiled=True)  12 us
    all_to_all x1, starting transfers between devices, per_device(): lax.all_to_all(spread, 'dev', split_axis=1, concat_axis=1, tiled=True)  11 us
  transfers between devices with their start and end apart: 3, of which 2 were waited for; matrix products, arithmetic and copies ran while one was open for 5% of the time, Pallas kernels for 0%

commit v1 on v0

v1 whole, which is shorter than its diff:
```python
import jax
import jax.numpy as jnp
from jax import lax
from jax.sharding import PartitionSpec as P

momentum_rate = 0.9
outer_rate = 0.7


def per_device(theta, deltas, momentum, basis, slot_matrix):
    matrices, rows, width = theta.shape
    slots, dev_count = momentum.shape[0], momentum.shape[1]
    piece = momentum.shape[3]
    rank = basis.shape[1]
    rep_count = lax.axis_size("rep")

    moment = momentum.reshape(slots, dev_count, piece * width).astype(jnp.bfloat16)
    landed = lax.all_to_all(moment, "dev", split_axis=1, concat_axis=1, tiled=True)

    compressed = jnp.dot(
        deltas[0].reshape(matrices * rows, width), basis, preferred_element_type=jnp.float32
    ).astype(jnp.bfloat16)
    every = lax.all_gather(compressed, "rep", axis=0, tiled=False)
    averaged = jnp.sum(every.astype(jnp.float32), axis=0) / rep_count
    high = averaged.astype(jnp.bfloat16)
    low = (averaged - high.astype(jnp.float32)).astype(jnp.bfloat16)
    outer = jnp.dot(
        jnp.concatenate([high, low], axis=1),
        jnp.concatenate([basis, basis], axis=1).T,
        preferred_element_type=jnp.float32,
    ).reshape(matrices, rows, width)

    paired_match = slot_matrix[None, :] == jnp.arange(matrices, dtype=jnp.int32)[:, None]
    slot_position = jnp.sum(
        jnp.where(paired_match, jnp.arange(slots * dev_count, dtype=jnp.int32)[None, :], 0), axis=1
    )
    ordering = slot_position % slots * dev_count + slot_position // slots
    chosen = jnp.take(landed.reshape(slots * dev_count, piece * width), ordering, axis=0)
    spread = lax.all_gather(chosen.reshape(matrices, 1, piece * width), "rep", axis=1, tiled=True)
    moments = spread.reshape(matrices, rows, width).astype(jnp.float32)
    renewed = momentum_rate * moments + outer
    update = (outer_rate * (outer + momentum_rate * renewed)).astype(jnp.bfloat16)
    return (theta.astype(jnp.float32) - update.astype(jnp.float32)).astype(jnp.bfloat16)


def solution(mesh):
    placed = (
        P(None, "dev", None),
        P("rep", None, "dev", None),
        P("dev", None, "rep", None, None),
        P(),
        P(),
    )
    return jax.shard_map(
        per_device, mesh=mesh, in_specs=placed, out_specs=P(None, "dev", None), check_vma=False
    )
```

time: 541 us -> 183 us (0.34)
  waiting for transfers between devices: 359 us -> 72.5 us
  local copies, waits for them, and re-layouts: 80.1 us -> 36 us
  blocking collectives: 34.4 us -> 14.5 us
    all_to_all x1, waiting for transfers between devices: 250 us -> 66.5 us  [per_device(): lax.all_to_all(moment, 'dev', split_axis=1, concat_axis=1, tiled=True)]
    all_gather x1, waiting for transfers between devices: 109 us -> 6.06 us  [per_device(): lax.all_gather(chosen.reshape(matrices, 1, piece * width), 'rep', axis=1,...]
    all_to_all x1 -> x0, blocking collectives: 34.4 us -> none  [per_device(): lax.all_to_all(outgoing, 'dev', split_axis=1, concat_axis=1, tiled=True)]
    all_gather x1 -> x0, local copies, waits for them, and re-layouts: 22 us -> none  [per_device(): lax.all_gather(update.reshape(slots, dev_count, 1, piece, width), 'rep',...]
    mul x2 -> x1, other arithmetic: 22.3 us -> 2.05 us  [per_device(): renewed = momentum_rate * moments + outer]
    reshape x3 -> x1, local copies, waits for them, and re-layouts: 24.9 us -> 4.95 us  [per_device(): outer = jnp.dot(jnp.concatenate([high, low], axis=1), jnp.concatenate([ba...]
    convert_element_type x2 -> x3, other arithmetic: 6.01 us -> 24.3 us  [the longest x1 18.4 us: per_device(): momentum.reshape(slots, dev_count, piece * width).astype(jnp.bfloat16)]
    all_gather x0 -> x1, blocking collectives: none -> 14.5 us  [per_device(): every = lax.all_gather(compressed, 'rep', axis=0, tiled=False)]
  transfers between devices with their start and end apart: 3 -> 2, of which waited for: 2 -> 2; matrix products, arithmetic and copies ran while one was open for 5% -> 8% of each run, Pallas kernels for 0% -> 0%
where the time goes in v1:
time: 183 us; the launch traced here: 182 us
  waiting for transfers between devices  72.5 us (40%)
  local copies, waits for them, and re-layouts  36 us (20%)
  other arithmetic  27.5 us (15%)
  blocking collectives  14.5 us (8%)
  between operations  13.5 us (7%)
  starting transfers between devices  13.2 us (7%)
  matrix products  5.22 us (3%)
    all_to_all x1, waiting for transfers between devices, per_device(): lax.all_to_all(moment, 'dev', split_axis=1, concat_axis=1, tiled=True)  66.5 us
    convert_element_type x1, other arithmetic, per_device(): momentum.reshape(slots, dev_count, piece * width).astype(jnp.bfloat16)  18.4 us
    all_gather x1, blocking collectives, per_device(): every = lax.all_gather(compressed, 'rep', axis=0, tiled=False)  14.5 us
    all_to_all x1, starting transfers between devices, per_device(): lax.all_to_all(moment, 'dev', split_axis=1, concat_axis=1, tiled=True)  13.2 us
    mul x2, local copies, waits for them, and re-layouts, per_device(): renewed = momentum_rate * moments + outer  11.1 us
    convert_element_type x2, local copies, waits for them, and re-layouts, per_device(): momentum.reshape(slots, dev_count, piece * width).astype(jnp.bfloat16)  9.38 us
    all_gather x1, waiting for transfers between devices, per_device(): lax.all_gather(chosen.reshape(matrices, 1, piece * width), 'rep', axis=1,...  6.06 us
    convert_element_type x1, other arithmetic, per_device(): (theta.astype(jnp.float32) - update.astype(jnp.float32)).astype(jnp.bfloa...  5.8 us
  transfers between devices with their start and end apart: 2, of which 2 were waited for; matrix products, arithmetic and copies ran while one was open for 8% of the time, Pallas kernels for 0%

profile of v1, /device:TPU:1, one launch (start us, length us, event | category | flops | bytes accessed | tf_op | source)
XLA Modules:
  0.0 182.4 jit_solution(10719013002869826443)
XLA Ops:
  6.5 18.4 %convert_reduce_fusion = bf16[2,64,11,1024]{3,2,1,0:T(8,128)(2,1)} fusion(f32[2,64,1,11,1024]{4,2,3,1,0:T(1,128)} %param.7), kind=kLoop, calls=%fused_computation.1 | loop fusion | flops 1441792 | bytes 8650752 | tf_op jit(solution)/shard_map/convert_element_type | solution.py:17
  25.0 4.8 %convert_element_type.44 = bf16[2,64,11264]{2,1,0:T(8,128)(2,1)S(1)} reshape(bf16[2,64,11,1024]{3,2,1,0:T(8,128)(2,1)} %convert_reduce_fusion) | data formatting | bytes 5767168 | tf_op jit(solution)/shard_map/convert_element_type | solution.py:17
  29.8 0.0 copy-start.2
  29.8 4.6 %copy.26 = bf16[2,64,11264]{2,0,1:T(2,128)(2,1)} copy(bf16[2,64,11264]{2,1,0:T(8,128)(2,1)S(1)} %convert_element_type.44) | data formatting | bytes 5767168 | tf_op jit(solution)/shard_map/convert_element_type | solution.py:17
  34.4 13.2 %all-to-all-start = ((bf16[2,64,11264]{2,0,1:T(2,128)(2,1)}), bf16[2,64,11264]{2,0,1:T(2,128)(2,1)}, u32[]{:S(2)}, u32[]{:S(2)}) async-start(bf16[2,64,11264]{2,0,1:T(2,128)(2,1)} %copy.26), calls=%async_computation | async-start | bytes 5767168 | tf_op jit(solution)/shard_map/all_to_all | solution.py:18
  47.5 0.0 all-gather.4.cloned.1.call-start
  47.6 0.0 copy-done.2
  47.6 0.1 select_reduce_fusion
  47.7 66.5 %all-to-all-done = bf16[2,64,11264]{2,0,1:T(2,128)(2,1)} async-done(((bf16[2,64,11264]{2,0,1:T(2,128)(2,1)}), bf16[2,64,11264]{2,0,1:T(2,128)(2,1)}, u32[]{:S(2)}, u32[]{:S(2)}) %all-to-all-start) | async-done | bytes 2883616 | tf_op jit(solution)/shard_map/all_to_all | solution.py:18
  114.2 2.4 %copy.27 = bf16[2,64,11264]{2,1,0:T(8,128)(2,1)S(1)} copy(bf16[2,64,11264]{2,0,1:T(2,128)(2,1)} %all-to-all-done) | data formatting | bytes 5767168 | tf_op jit(solution)/shard_map/all_to_all | solution.py:18
  116.6 0.9 gather_fusion
  117.5 0.9 bitcast_select_fusion
  118.4 0.0 all-gather.4.cloned.1.call-update
  118.4 0.0 copy-start.1
  118.4 2.8 %copy.25 = bf16[1,24,44,1024]{3,2,1,0:T(8,128)(2,1)S(1)} copy(bf16[1,24,44,1024]{3,1,2,0:T(8,128)(2,1)} %param.6) | data formatting | bytes 4325376 | tf_op args[1]
  121.3 2.0 %reshape_squeeze.3 = bf16[1056,1024]{1,0:T(8,128)(2,1)} reshape(bf16[1,24,44,1024]{3,2,1,0:T(8,128)(2,1)S(1)} %copy.25) | data formatting | bytes 4325376 | tf_op jit(solution)/shard_map/reshape;squeeze | solution.py:21
  123.3 0.0 copy-done.1
  123.3 2.4 %fusion = bf16[1,1056,64]{1,2,0:T(8,128)(2,1)S(1)} fusion(bf16[1056,1024]{1,0:T(8,128)(2,1)} %reshape_squeeze.3, bf16[1024,64]{0,1:T(8,128)(2,1)S(1)} %copy-done.1), kind=kOutput, calls=%fused_computation.6 | convolution fusion | flops 138479616 | bytes 2428928 | tf_op jit(solution)/shard_map/dot_general | solution.py:20
  125.7 14.5 %all-gather.1 = bf16[4,1056,64]{1,2,0:T(8,128)(2,1)S(1)} all-gather(bf16[1,1056,64]{1,2,0:T(8,128)(2,1)S(1)} %fusion), channel_id=2, replica_groups=mesh['rep'=4,'dev'=64] {'rep'}, dimensions={0}, use_global_device_ids=true | all-gather | bytes 675840 | tf_op jit(solution)/shard_map/all_gather | solution.py:23
  140.2 0.1 convert_reduce_fusion.1
  140.3 2.8 %fusion.1 = f32[1056,1024]{1,0:T(8,128)} fusion(bf16[1056,64]{0,1:T(8,128)(2,1)S(1)} %get-tuple-element.6, bf16[1056,64]{0,1:T(8,128)(2,1)S(1)} %get-tuple-element.5, bf16[1024,64]{0,1:T(8,128)(2,1)S(1)} %copy-done.1), kind=kOutput, calls=%fused_computation.9 | convolution fusion | flops 277889024 | bytes 4726784 | tf_op jit(solution)/shard_map/dot_general | solution.py:27
  143.1 5.0 %reshape.125 = f32[24,44,1024]{2,1,0:T(8,128)} reshape(f32[1056,1024]{1,0:T(8,128)} %fusion.1) | data formatting | bytes 8650752 | tf_op jit(solution)/shard_map/reshape | solution.py:31
  148.1 6.1 %all-gather.4.cloned.1.call-done = bf16[24,4,11264]{2,0,1:T(8,128)(2,1)} async-done(((bf16[24,1,11264]{2,0,1:T(8,128)(2,1)}), bf16[24,4,11264]{2,0,1:T(8,128)(2,1)}) %all-gather.4.cloned.1.call-update) | async-done | bytes 2162704 | tf_op jit(solution)/shard_map/all_gather | solution.py:39
  154.1 2.1 %convert_multiply_fusion = f32[24,4,11264]{2,0,1:T(8,128)S(1)} fusion(bf16[24,4,11264]{2,0,1:T(8,128)(2,1)} %all-gather.4.cloned.1.call-done), kind=kLoop, calls=%fused_computation.4 | loop fusion | flops 2162688 | bytes 6488064 | tf_op jit(solution)/shard_map/mul | solution.py:41
  156.2 4.9 %copy.28 = f32[24,4,11264]{2,1,0:T(4,128)} copy(f32[24,4,11264]{2,0,1:T(8,128)S(1)} %convert_multiply_fusion) | data formatting | bytes 8650752 | tf_op jit(solution)/shard_map/mul | solution.py:41
  161.1 0.0 copy-start
  161.1 6.2 %mul.32 = f32[24,44,1024]{2,1,0:T(8,128)} reshape(f32[24,4,11264]{2,1,0:T(4,128)} %copy.28) | data formatting | bytes 8650752 | tf_op jit(solution)/shard_map/mul | solution.py:41
  167.3 0.0 copy-done
  167.3 5.8 %subtract_convert_fusion = bf16[24,44,1024]{2,1,0:T(8,128)(2,1)S(1)} fusion(f32[24,44,1024]{2,1,0:T(8,128)} %reshape.125, f32[24,44,1024]{2,1,0:T(8,128)} %mul.32, bf16[24,44,1024]{2,0,1:T(8,128)(2,1)S(1)} %copy-done), kind=kLoop, calls=%fused_computation.2 | loop fusion | flops 9732096 | bytes 12976128 | tf_op jit(solution)/shard_map/convert_element_type | solution.py:43
  173.1 2.5 %copy.29 = bf16[24,44,1024]{2,0,1:T(8,128)(2,1)} copy(bf16[24,44,1024]{2,1,0:T(8,128)(2,1)S(1)} %subtract_convert_fusion) | data formatting | bytes 4325376 | tf_op jit(solution)/shard_map/convert_element_type | solution.py:43
  (4 shorter events, 0.1 us)
Async XLA Ops:
  29.8 17.8 %copy-start.2 = (s32[128]{0:T(128)S(1)}, s32[128]{0:T(128)}, u32[]{:S(2)}) copy-start(s32[128]{0:T(128)} %param.9) | copy-start | bytes 1540
  34.4 79.8 %all-to-all-start = ((bf16[2,64,11264]{2,0,1:T(2,128)(2,1)}), bf16[2,64,11264]{2,0,1:T(2,128)(2,1)}, u32[]{:S(2)}, u32[]{:S(2)}) async-start(bf16[2,64,11264]{2,0,1:T(2,128)(2,1)} %copy.26), calls=%async_computation | async-start | bytes 5767168 | tf_op jit(solution)/shard_map/all_to_all | solution.py:18
  47.5 106.6 %all-gather.4.cloned.1.call-start = ((), (), s32[]{:S(2)}) async-start(), calls=%async_computation.1 | async-start | bytes 2703360 | tf_op jit(solution)/shard_map/all_gather | solution.py:39
  118.4 4.9 %copy-start.1 = (bf16[1024,64]{0,1:T(8,128)(2,1)S(1)}, bf16[1024,64]{0,1:T(8,128)(2,1)}, u32[]{:S(2)}) copy-start(bf16[1024,64]{0,1:T(8,128)(2,1)} %param.8) | copy-start | bytes 393220
  161.1 6.2 %copy-start = (bf16[24,44,1024]{2,0,1:T(8,128)(2,1)S(1)}, bf16[24,44,1024]{2,0,1:T(8,128)(2,1)}, u32[]{:S(2)}) copy-start(bf16[24,44,1024]{2,0,1:T(8,128)(2,1)} %param.5) | copy-start | bytes 6488068
Sparse Core Ops, SparseCore 0:
  118.5 35.5 all-gather.3

commit v2 on v1

v2 whole, which is shorter than its diff:
```python
import functools

import jax
import jax.numpy as jnp
from jax import lax
from jax.experimental import pallas as pl
from jax.experimental.pallas import tpu as pltpu
from jax.sharding import PartitionSpec as P

momentum_rate = 0.9
outer_rate = 0.7
MESH = pl.DeviceIdType.MESH
ROW = 8
DEPTH = 8
REPS = 4
CHUNKS = ((0, 3), (3, 3), (6, 3), (9, 2))


def route(
    cap, row_ref, pick_ref, mom_ref, deltas_ref, basis_ref, moments_ref, comp_ref,
    row_in, z_out, z_in, copy_sems, x_send, x_recv, z_send, z_recv, y_send, y_recv, c_send, c_recv,
):
    rep = lax.axis_index("rep")
    dev = lax.axis_index("dev")
    z, place = dev // ROW, lax.rem(dev, ROW)
    slots = mom_ref.shape[0]
    right, left = lax.rem(rep + 1, REPS), lax.rem(rep + 3, REPS)
    across = lax.rem(rep + 2, REPS)

    def row_peer(step):
        return lax.rem(place + step, ROW)

    def z_peer(step):
        return lax.rem(z + step, DEPTH)

    barrier = pltpu.get_barrier_semaphore()
    for step in range(1, ROW):
        pl.semaphore_signal(barrier, inc=1, device_id=(rep, z * ROW + row_peer(step)), device_id_type=MESH)
    for step in range(1, DEPTH):
        pl.semaphore_signal(barrier, inc=1, device_id=(rep, z_peer(step) * ROW + place), device_id_type=MESH)
    for peer in (right, left, across):
        pl.semaphore_signal(barrier, inc=1, device_id=(peer, dev), device_id_type=MESH)
    pl.semaphore_wait(barrier, ROW + DEPTH + 1)

    def x_copy(chunk, step):
        start, count = CHUNKS[chunk]
        return pltpu.make_async_remote_copy(
            src_ref=mom_ref.at[:, :, row_peer(step), pl.ds(start, count)],
            dst_ref=row_in[chunk].at[pl.ds(place * slots, slots)],
            send_sem=x_send.at[chunk, step - 1],
            recv_sem=x_recv.at[chunk, step - 1],
            device_id=(rep, z * ROW + row_peer(step)),
            device_id_type=MESH,
        )

    def own_copy(chunk):
        start, count = CHUNKS[chunk]
        return pltpu.make_async_copy(
            mom_ref.at[:, :, place, pl.ds(start, count)],
            row_in[chunk].at[pl.ds(place * slots, slots)],
            copy_sems.at[chunk],
        )

    def z_copy(chunk, step):
        return pltpu.make_async_remote_copy(
            src_ref=z_out[chunk].at[z_peer(step)],
            dst_ref=z_in[chunk].at[pl.ds(z * cap, cap)],
            send_sem=z_send.at[chunk, step - 1],
            recv_sem=z_recv.at[chunk, step - 1],
            device_id=(rep, z_peer(step) * ROW + place),
            device_id_type=MESH,
        )

    def y_copy(chunk, way, block, target):
        start, count = CHUNKS[chunk]
        return pltpu.make_async_remote_copy(
            src_ref=moments_ref.at[block, pl.ds(start, count)],
            dst_ref=moments_ref.at[block, pl.ds(start, count)],
            send_sem=y_send.at[chunk, way],
            recv_sem=y_recv.at[chunk, way],
            device_id=(target, dev),
            device_id_type=MESH,
        )

    def to_right(chunk):
        return y_copy(chunk, 0, rep, right)

    def to_left(chunk):
        return y_copy(chunk, 1, rep, left)

    def onward(chunk):
        if chunk % 2 == 0:
            return y_copy(chunk, 2, left, right)
        return y_copy(chunk, 2, right, left)

    def c_copy(way, target):
        return pltpu.make_async_remote_copy(
            src_ref=comp_ref.at[rep],
            dst_ref=comp_ref.at[rep],
            send_sem=c_send.at[way],
            recv_sem=c_recv.at[way],
            device_id=(target, dev),
            device_id_type=MESH,
        )

    for chunk in range(len(CHUNKS)):
        for step in range(1, ROW):
            x_copy(chunk, step).start()
        own_copy(chunk).start()

    half = comp_ref.shape[1]
    basis = basis_ref[...]
    nothing = jnp.zeros_like(basis)
    dims = (((1,), (1,)), ((), ()))
    comp_ref[rep] = (
        lax.dot_general(deltas_ref[:half], jnp.concatenate([basis, nothing], axis=0), dims, preferred_element_type=jnp.float32)
        + lax.dot_general(deltas_ref[half:], jnp.concatenate([nothing, basis], axis=0), dims, preferred_element_type=jnp.float32)
    ).astype(jnp.bfloat16)
    for way, target in enumerate((right, left, across)):
        c_copy(way, target).start()

    def stage_z(chunk):
        for step in range(1, ROW):
            x_copy(chunk, step).wait_recv()
        own_copy(chunk).wait()
        for slot in range(cap):
            z_out[chunk][:, slot] = row_in[chunk][row_ref[slot]]
        for step in range(1, DEPTH):
            z_copy(chunk, step).start()
        z_in[chunk][pl.ds(z * cap, cap)] = z_out[chunk][z]

    def stage_y(chunk):
        start, count = CHUNKS[chunk]
        for step in range(1, DEPTH):
            z_copy(chunk, step).wait_recv()
        for group in range(moments_ref.shape[2]):
            for line in range(count):
                tile = jnp.stack(
                    [z_in[chunk][pick_ref[group * 8 + m], line].astype(jnp.float32) for m in range(8)], axis=0
                )
                moments_ref[rep, start + line, group] = jnp.swapaxes(tile, 0, 1).astype(jnp.bfloat16)
        to_right(chunk).start()
        to_left(chunk).start()

    def stage_relay(chunk):
        if chunk % 2 == 0:
            to_right(chunk).wait_recv()
        else:
            to_left(chunk).wait_recv()
        onward(chunk).start()

    def stage_end(chunk):
        if chunk % 2 == 0:
            to_left(chunk).wait_recv()
        else:
            to_right(chunk).wait_recv()
        onward(chunk).wait_recv()

    total = len(CHUNKS)
    for tick in range(total + 2):
        if tick < total:
            stage_z(tick)
        if 0 <= tick - 1 < total:
            stage_y(tick - 1)
        if 0 <= tick - 2 < total:
            stage_relay(tick - 2)
    for way, target in enumerate((right, left, across)):
        c_copy(way, target).wait()
    for chunk in range(total):
        stage_end(chunk)
    for chunk in range(total):
        for step in range(1, ROW):
            x_copy(chunk, step).wait_send()
        for step in range(1, DEPTH):
            z_copy(chunk, step).wait_send()
        to_right(chunk).wait_send()
        to_left(chunk).wait_send()
        onward(chunk).wait_send()


def routed(cap, row_slots, picks, moment, deltas, basis_t):
    slots, _, _, piece, tiles, lanes = moment.shape
    matrices = picks.shape[0]
    rank = basis_t.shape[0]
    half = deltas.shape[0] // 2
    chunks = len(CHUNKS)
    smem = pl.BlockSpec(memory_space=pltpu.SMEM)
    vmem = pl.BlockSpec(memory_space=pltpu.VMEM)
    return pl.pallas_call(
        functools.partial(route, cap),
        name="route_%d" % cap,
        out_shape=(
            jax.ShapeDtypeStruct((REPS, piece, matrices // 8, tiles, 8, lanes), jnp.bfloat16),
            jax.ShapeDtypeStruct((REPS, half, 2 * rank), jnp.bfloat16),
        ),
        in_specs=[smem, smem, pl.BlockSpec(memory_space=pl.ANY), vmem, vmem],
        out_specs=(vmem, vmem),
        scratch_shapes=[
            [pltpu.VMEM((ROW * slots, DEPTH, n, tiles, lanes), jnp.bfloat16) for _, n in CHUNKS],
            [pltpu.VMEM((DEPTH, cap, n, tiles, lanes), jnp.bfloat16) for _, n in CHUNKS],
            [pltpu.VMEM((DEPTH * cap, n, tiles, lanes), jnp.bfloat16) for _, n in CHUNKS],
            pltpu.SemaphoreType.DMA((chunks,)),
            pltpu.SemaphoreType.DMA((chunks, ROW - 1)),
            pltpu.SemaphoreType.DMA((chunks, ROW - 1)),
            pltpu.SemaphoreType.DMA((chunks, DEPTH - 1)),
            pltpu.SemaphoreType.DMA((chunks, DEPTH - 1)),
            pltpu.SemaphoreType.DMA((chunks, 3)),
            pltpu.SemaphoreType.DMA((chunks, 3)),
            pltpu.SemaphoreType.DMA((3,)),
            pltpu.SemaphoreType.DMA((3,)),
        ],
        compiler_params=pltpu.CompilerParams(
            collective_id=cap, has_side_effects=True, vmem_limit_bytes=40 << 20
        ),
    )(row_slots, picks, moment, deltas, basis_t)


def narrow(wide_ref, narrow_ref):
    narrow_ref[...] = wide_ref[...].astype(jnp.bfloat16)


def narrowed(wide):
    rows, lanes = wide.shape
    steps = 8
    spec = pl.BlockSpec((rows // steps, lanes), lambda i: (i, 0))
    return pl.pallas_call(
        narrow,
        name="narrow",
        grid=(steps,),
        out_shape=jax.ShapeDtypeStruct(wide.shape, jnp.bfloat16),
        in_specs=[spec],
        out_specs=spec,
    )(wide)


def finish(theta_ref, moments_ref, comp_ref, basis_ref, out_ref):
    block = pl.program_id(0)
    piece, matrices, width = theta_ref.shape
    lanes = moments_ref.shape[-1]
    rows = piece * matrices
    start = pl.multiple_of(lax.rem(block, 2) * rows, 8)
    total = comp_ref[0, pl.ds(start, rows)].astype(jnp.float32)
    for rep in range(1, REPS):
        total += comp_ref[rep, pl.ds(start, rows)].astype(jnp.float32)
    averaged = total / REPS
    high = averaged.astype(jnp.bfloat16)
    low = (averaged - high.astype(jnp.float32)).astype(jnp.bfloat16)
    basis = basis_ref[block // 2]
    for tile in range(width // lanes):
        cut = pl.ds(tile * lanes, lanes)
        outer = jnp.dot(high, basis[:, tile * lanes:(tile + 1) * lanes], preferred_element_type=jnp.float32)
        outer += jnp.dot(low, basis[:, tile * lanes:(tile + 1) * lanes], preferred_element_type=jnp.float32)
        outer = outer.reshape(piece, matrices, lanes)
        moment = moments_ref[0, :, :, tile].astype(jnp.float32).reshape(piece, matrices, lanes)
        renewed = momentum_rate * moment + outer
        update = (outer_rate * (outer + momentum_rate * renewed)).astype(jnp.bfloat16)
        out_ref[:, :, cut] = (
            theta_ref[:, :, cut].astype(jnp.float32) - update.astype(jnp.float32)
        ).astype(jnp.bfloat16)


def finished(theta, moments, compressed, basis_pair):
    rows, matrices, width = theta.shape
    piece = rows // REPS
    return pl.pallas_call(
        finish,
        name="finish",
        grid=(REPS,),
        out_shape=jax.ShapeDtypeStruct(theta.shape, jnp.bfloat16),
        in_specs=[
            pl.BlockSpec((piece, matrices, width), lambda r: (r, 0, 0)),
            pl.BlockSpec((1,) + moments.shape[1:], lambda r: (r, 0, 0, 0, 0, 0)),
            pl.BlockSpec(compressed.shape, lambda r: (0, 0, 0)),
            pl.BlockSpec(basis_pair.shape, lambda r: (0, 0, 0)),
        ],
        out_specs=pl.BlockSpec((piece, matrices, width), lambda r: (r, 0, 0)),
    )(theta, moments, compressed, basis_pair)


def per_device(caps, theta, deltas, momentum, basis, slot_matrix):
    matrices, rows, width = theta.shape
    slots, dev_count = momentum.shape[0], momentum.shape[1]
    piece = momentum.shape[3]
    entries = slots * dev_count
    per_row = slots * ROW

    moment = narrowed(momentum.reshape(-1, 128)).reshape(slots, DEPTH, ROW, piece, width // 128, 128)
    by_row = deltas[0].transpose(1, 0, 2).reshape(rows * matrices, width)
    basis_t = basis.T
    nothing = jnp.zeros_like(basis_t)
    basis_pair = jnp.stack(
        [jnp.concatenate([basis_t, nothing], axis=0), jnp.concatenate([nothing, basis_t], axis=0)]
    )

    place = jnp.arange(entries, dtype=jnp.int32)
    filled = slot_matrix >= 0
    ahead = (place[None, :] // per_row == place[:, None] // per_row) & (place[None, :] < place[:, None])
    order = jnp.sum((ahead & filled[None, :]).astype(jnp.int32), axis=1)
    mine = filled & (place // per_row == lax.axis_index("dev") // ROW)
    row_slots = jnp.sum(
        jnp.where(mine[None, :] & (order[None, :] == jnp.arange(per_row, dtype=jnp.int32)[:, None]), place % per_row, 0), axis=1
    )
    match = slot_matrix[None, :] == jnp.arange(matrices, dtype=jnp.int32)[:, None]
    owner_row = jnp.sum(jnp.where(match, place // per_row, 0), axis=1)
    owner_order = jnp.sum(jnp.where(match, order, 0), axis=1)
    largest = jnp.max(jnp.where(filled, order, 0)) + 1

    def branch(cap):
        return lambda: routed(cap, row_slots[:cap], owner_row * cap + owner_order, moment, by_row, basis_t)

    if len(caps) == 1:
        moments, compressed = branch(caps[0])()
    else:
        which = sum((largest > cap).astype(jnp.int32) for cap in caps[:-1])
        moments, compressed = lax.switch(which, [branch(cap) for cap in caps])
    return finished(theta.transpose(1, 0, 2), moments, compressed, basis_pair).transpose(1, 0, 2)


def solution(mesh):
    placed = (
        P(None, "dev", None),
        P("rep", None, "dev", None),
        P("dev", None, "rep", None, None),
        P(),
        P(),
    )
    return jax.shard_map(
        functools.partial(per_device, (6, 16)),
        mesh=mesh, in_specs=placed, out_specs=P(None, "dev", None), check_vma=False,
    )
```

time: 183 us -> 80.4 us (0.44)
  Pallas kernels: 0 us -> 75.5 us
  waiting for transfers between devices: 72.5 us -> 0 us
  local copies, waits for them, and re-layouts: 36 us -> 0.6 us
  other arithmetic: 27.5 us -> 3.22 us
  blocking collectives: 14.5 us -> 0 us
  starting transfers between devices: 13.2 us -> 0 us
  between operations: 13.5 us -> 0.73 us
  matrix products: 5.22 us -> 0 us
    pallas_call x0 -> x3, Pallas kernels: none -> 75.5 us  [the longest x1 64.5 us: routed(): pl.pallas_call(functools.partial(route, cap), name='route_%d' % cap, out_...]
    all_to_all x1 -> x0, waiting for transfers between devices: 66.5 us -> none  [per_device(): lax.all_to_all(moment, 'dev', split_axis=1, concat_axis=1, tiled=True)]
    convert_element_type x3 -> x0, other arithmetic: 24.3 us -> none  [the longest x1 18.4 us: per_device(): momentum.reshape(slots, dev_count, piece * width).astype(jnp.bfloat16)]
    all_gather x1 -> x0, blocking collectives: 14.5 us -> none  [per_device(): every = lax.all_gather(compressed, 'rep', axis=0, tiled=False)]
    all_to_all x1 -> x0, starting transfers between devices: 13.2 us -> none  [per_device(): lax.all_to_all(moment, 'dev', split_axis=1, concat_axis=1, tiled=True)]
    convert_element_type x3 -> x0, local copies, waits for them, and re-layouts: 11.9 us -> none  [the longest x2 9.38 us: per_device(): momentum.reshape(slots, dev_count, piece * width).astype(jnp.bfloat16)]
    mul x2 -> x0, local copies, waits for them, and re-layouts: 11.1 us -> none  [per_device(): renewed = momentum_rate * moments + outer]
    all_gather x1 -> x0, waiting for transfers between devices: 6.06 us -> none  [per_device(): lax.all_gather(chosen.reshape(matrices, 1, piece * width), 'rep', axis=1,...]
  transfers between devices with their start and end apart: 2 -> 0, of which waited for: 2 -> 0; matrix products, arithmetic and copies ran while one was open for 8% -> 0% of each run, Pallas kernels for 0% -> 0%
where the time goes in v2:
time: 80.4 us; the launch traced here: 80.1 us
  Pallas kernels  75.5 us (94%)
  other arithmetic  3.22 us (4%)
    pallas_call x1, Pallas kernels, routed(): pl.pallas_call(functools.partial(route, cap), name='route_%d' % cap, out_...  64.5 us
    pallas_call x1, Pallas kernels, finished(): pl.pallas_call(finish, name='finish', grid=(REPS,), out_shape=jax.ShapeDt...  5.99 us
    pallas_call x1, Pallas kernels, narrowed(): pl.pallas_call(narrow, name='narrow', grid=(steps,), out_shape=jax.ShapeD...  5.01 us

profile of v2, /device:TPU:1, one launch (start us, length us, event | category | flops | bytes accessed | tf_op | source)
XLA Modules:
  0.0 80.1 jit_solution(15418300737068781643)
XLA Ops:
  0.0 0.7 compare_and_fusion
  0.7 0.2 convert_reduce_fusion
  0.9 0.1 select_reduce_fusion.2
  1.0 0.8 select_reduce_fusion
  1.7 0.0 copy-start.3
  1.8 0.0 copy-start
  1.8 5.0 %narrow.1 = bf16[11264,128]{1,0:T(8,128)(2,1)S(1)} custom-call(f32[11264,128]{1,0:T(8,128)} %bitcast.19), custom_call_target="tpu_custom_call" | custom-call | tf_op jit(solution)/shard_map/narrow/pallas_call | solution.py:226
  6.8 0.0 copy-done.3
  6.8 0.6 select_reduce_fusion.3
  8.1 0.0 copy-done
  8.1 65.1 %conditional.1 = ((bf16[4,11,3,8,8,128]{5,4,3,2,1,0:T(8,128)(2,1)}, bf16[4,528,128]{2,1,0:T(8,128)(2,1)S(1)})) conditional(s32[]{:T(128)} %clamp.3, (s32[16]{0:T(128)S(1)}, s32[24]{0:T(128)S(1)}, s32[24]{0:T(128)S(1)}, bf16[2,8,8,11,8,128]{5,4,3,2,1,0:T(8,128)(2,1)S(1)}, bf16[1056,1024]{1,0:T(8,128)(2,1)}, ...), branch_computations={%region_5.6_spmd, %region_6.7_spmd} | conditional | flops 48 | bytes 580 | solution.py:315
  8.1 0.0 copy-start.1
  8.1 0.5 copy-done.1
  8.7 64.5 %route_6.1 = (bf16[4,11,3,8,8,128]{5,4,3,2,1,0:T(8,128)(2,1)}, bf16[4,528,128]{2,1,0:T(8,128)(2,1)S(1)}) custom-call(s32[6]{0:T(128)} %bitcast.24, s32[24]{0:T(128)S(1)} %multiply_add_fusion.pick_ref, bf16[2,8,8,11,8,128]{5,4,3,2,1,0:T(8,128)(2,1)S(1)} %get-tuple-element.32.mom_ref, bf16[1056,1024]{1,0:T(8,128)(2,1)} %get-tuple-element.33.deltas_ref, ...), custom_call_target="tpu_custom_call" | custom-call | tf_op jit(solution)/shard_map/cond/branch_0_fun/route_6/pallas_call | solution.py:189
  73.3 0.8 %pad_maximum_fusion.basis_ref = bf16[2,128,1024]{2,1,0:T(8,128)(2,1)} fusion(bf16[1,128,1024]{2,1,0:T(8,128)(2,1)S(1)} %get-tuple-element.48, bf16[1,128,1024]{2,1,0:T(8,128)(2,1)S(1)} %get-tuple-element.47), kind=kLoop, calls=%fused_computation.2 | loop fusion | flops 262144 | bytes 1048576 | tf_op jit(solution)/shard_map/stack | solution.py:291
  74.1 6.0 %finish.1 = bf16[44,24,1024]{2,1,0:T(8,128)(2,1)} custom-call(bf16[44,24,1024]{2,1,0:T(8,128)(2,1)} %bitcast.20, bf16[4,11,3,8,8,128]{5,4,3,2,1,0:T(8,128)(2,1)} %get-tuple-element.43.moments_ref, bf16[4,528,128]{2,1,0:T(8,128)(2,1)S(1)} %get-tuple-element.44.comp_ref, bf16[2,128,1024]{2,1,0:T(8,128)(2,1)} %pad_maximum_fusion.basis_ref), custom_call_target="tpu_custom_call" | custom-call | tf_op jit(solution)/shard_map/finish/pallas_call | solution.py:265
  (4 shorter events, 0.1 us)
Async XLA Ops:
  1.7 5.0 %copy-start.3 = (s32[128]{0:T(128)S(1)}, s32[128]{0:T(128)}, u32[]{:S(2)}) copy-start(s32[128]{0:T(128)} %param.11) | copy-start | bytes 1540
  1.8 6.3 %copy-start = (bf16[1024,64]{0,1:T(8,128)(2,1)S(1)}, bf16[1024,64]{0,1:T(8,128)(2,1)}, u32[]{:S(2)}) copy-start(bf16[1024,64]{0,1:T(8,128)(2,1)} %param.10) | copy-start | bytes 393220
  8.1 0.6 copy-start.1

commit v3 on v1

v3 whole, which is shorter than its diff:
```python
import functools

import jax
import jax.numpy as jnp
from jax import lax
from jax.experimental import pallas as pl
from jax.experimental.pallas import tpu as pltpu
from jax.sharding import PartitionSpec as P

momentum_rate = 0.9
outer_rate = 0.7
MESH = pl.DeviceIdType.MESH
CORES = 2
WIDE = 4
DEPTH = 8
REPS = 4
CHUNKS = ((0, 3), (3, 3), (6, 3), (9, 2))
CAPS = ((3, 6), (4, 8), (4, 16))


def route(
    chip_cap, row_cap, table_ref, mom_ref, deltas_ref, basis_ref, theta_ref, out_ref,
    wide, core_out, chip_in, x_out, row_in, z_out, z_in, moments, comp, deltas, theta, outer,
    load_sem, core_send, core_recv, x_send, x_recv, z_send, z_recv, y_send, y_recv, c_send, c_recv,
):
    rep = lax.axis_index("rep")
    dev = lax.axis_index("dev")
    core, x, z = lax.rem(dev, CORES), lax.rem(dev // CORES, WIDE), dev // (CORES * WIDE)
    slots = mom_ref.shape[0]
    total = len(CHUNKS)
    right, left, across = (lax.rem(rep + step, REPS) for step in (1, 3, 2))
    partner = (rep, dev + 1 - 2 * core)

    def x_peer(step):
        return lax.rem(x + step, WIDE)

    def x_device(step):
        return (rep, (z * WIDE + x_peer(step)) * CORES + core)

    def z_peer(step):
        return lax.rem(z + step, DEPTH)

    def z_device(step):
        return (rep, (z_peer(step) * WIDE + x) * CORES + core)

    def wide_copy(chunk):
        start, count = CHUNKS[chunk]
        return pltpu.make_async_copy(
            mom_ref.at[:, :, :, :, pl.ds(start, count)], wide[chunk], load_sem.at[chunk]
        )

    deltas_copy = pltpu.make_async_copy(deltas_ref, deltas, load_sem.at[total])
    theta_copy = pltpu.make_async_copy(theta_ref, theta, load_sem.at[total + 1])
    for chunk in range(total):
        wide_copy(chunk).start()
    deltas_copy.start()
    theta_copy.start()

    barrier = pltpu.get_barrier_semaphore()
    peers = [partner]
    peers += [x_device(step) for step in range(1, WIDE)]
    peers += [z_device(step) for step in range(1, DEPTH)]
    peers += [(peer, dev) for peer in (right, left, across)]
    for peer in peers:
        pl.semaphore_signal(barrier, inc=1, device_id=peer, device_id_type=MESH)

    def remote(src, dst, send, recv, device):
        return pltpu.make_async_remote_copy(
            src_ref=src, dst_ref=dst, send_sem=send, recv_sem=recv, device_id=device, device_id_type=MESH
        )

    def core_copy(chunk):
        return remote(
            core_out[chunk], chip_in[chunk].at[pl.ds(core * slots, slots)],
            core_send.at[chunk], core_recv.at[chunk], partner,
        )

    def x_copy(chunk, step):
        return remote(
            x_out[chunk].at[x_peer(step)], row_in[chunk].at[pl.ds(x * chip_cap, chip_cap)],
            x_send.at[chunk, step - 1], x_recv.at[chunk, step - 1], x_device(step),
        )

    def z_copy(chunk, step):
        return remote(
            z_out[chunk].at[z_peer(step)], z_in[chunk].at[pl.ds(z * row_cap, row_cap)],
            z_send.at[chunk, step - 1], z_recv.at[chunk, step - 1], z_device(step),
        )

    def y_copy(chunk, way, block, target):
        start, count = CHUNKS[chunk]
        part = moments.at[block, pl.ds(start, count)]
        return remote(part, part, y_send.at[chunk, way], y_recv.at[chunk, way], (target, dev))

    def to_right(chunk):
        return y_copy(chunk, 0, rep, right)

    def to_left(chunk):
        return y_copy(chunk, 1, rep, left)

    def onward(chunk):
        if chunk % 2 == 0:
            return y_copy(chunk, 2, left, right)
        return y_copy(chunk, 2, right, left)

    def c_copy(way):
        target = (right, left, across)[way]
        return remote(comp.at[rep], comp.at[rep], c_send.at[way], c_recv.at[way], (target, dev))

    def stage_core(chunk):
        wide_copy(chunk).wait()
        for column in range(WIDE):
            core_out[chunk][:, column] = wide[chunk][:, :, column, 1 - core].astype(jnp.bfloat16)
        if chunk == 0:
            pl.semaphore_wait(barrier, len(peers))
        core_copy(chunk).start()
        for column in range(WIDE):
            chip_in[chunk][pl.ds(core * slots, slots), column] = wide[chunk][:, :, column, core].astype(jnp.bfloat16)

    def stage_x(chunk):
        core_copy(chunk).wait_recv()
        for slot in range(chip_cap):
            x_out[chunk][:, slot] = chip_in[chunk][table_ref[slot]]
        for step in range(1, WIDE):
            x_copy(chunk, step).start()
        row_in[chunk][pl.ds(x * chip_cap, chip_cap)] = x_out[chunk][x]

    def stage_z(chunk):
        for step in range(1, WIDE):
            x_copy(chunk, step).wait_recv()
        for slot in range(row_cap):
            code = table_ref[4 + slot]
            z_out[chunk][:, slot] = row_in[chunk][code // 4 * chip_cap + lax.rem(code, 4)]
        for step in range(1, DEPTH):
            z_copy(chunk, step).start()
        z_in[chunk][pl.ds(z * row_cap, row_cap)] = z_out[chunk][z]

    def stage_y(chunk):
        start, count = CHUNKS[chunk]
        for step in range(1, DEPTH):
            z_copy(chunk, step).wait_recv()
        for group in range(moments.shape[2]):
            codes = [table_ref[20 + group * 8 + m] for m in range(8)]
            picks = [code // 16 * row_cap + lax.rem(code, 16) for code in codes]
            for line in range(count):
                tile = jnp.stack([z_in[chunk][pick, line].astype(jnp.float32) for pick in picks], axis=0)
                moments[rep, start + line, group] = jnp.swapaxes(tile, 0, 1).astype(jnp.bfloat16)
        to_right(chunk).start()
        to_left(chunk).start()

    def stage_relay(chunk):
        if chunk % 2 == 0:
            to_right(chunk).wait_recv()
        else:
            to_left(chunk).wait_recv()
        onward(chunk).start()

    def stage_end(chunk):
        if chunk % 2 == 0:
            to_left(chunk).wait_recv()
        else:
            to_right(chunk).wait_recv()
        onward(chunk).wait_recv()
        start, count = CHUNKS[chunk]
        piece, matrices, lanes = moments.shape[1], theta.shape[1], moments.shape[-1]
        for block in range(REPS):
            lines = pl.ds(block * piece + start, count)
            for tile in range(moments.shape[3]):
                cut = pl.ds(tile * lanes, lanes)
                moment = moments[block, pl.ds(start, count), :, tile].astype(jnp.float32)
                moment = moment.reshape(count, matrices, lanes)
                grad = outer[lines, :, cut]
                renewed = momentum_rate * moment + grad
                update = (outer_rate * (grad + momentum_rate * renewed)).astype(jnp.bfloat16)
                out_ref[lines, :, cut] = (
                    theta[lines, :, cut].astype(jnp.float32) - update.astype(jnp.float32)
                ).astype(jnp.bfloat16)

    half = comp.shape[1]

    def project():
        deltas_copy.wait()
        basis = basis_ref[...]
        nothing = jnp.zeros_like(basis)
        dims = (((1,), (1,)), ((), ()))
        upper = jnp.concatenate([basis, nothing], axis=0)
        lower = jnp.concatenate([nothing, basis], axis=0)
        comp[rep] = (
            lax.dot_general(deltas[:half], upper, dims, preferred_element_type=jnp.float32)
            + lax.dot_general(deltas[half:], lower, dims, preferred_element_type=jnp.float32)
        ).astype(jnp.bfloat16)
        for way in range(3):
            c_copy(way).start()

    def expand():
        for way in range(3):
            c_copy(way).wait()
        theta_copy.wait()
        summed = comp[0].astype(jnp.float32)
        for block in range(1, REPS):
            summed += comp[block].astype(jnp.float32)
        averaged = summed / REPS
        high = averaged.astype(jnp.bfloat16)
        low = (averaged - high.astype(jnp.float32)).astype(jnp.bfloat16)
        both = jnp.concatenate([high, low], axis=1)
        basis = basis_ref[...]
        nothing = jnp.zeros_like(basis)
        rows, matrices, width = theta.shape
        for part in range(2):
            pair = [basis, nothing] if part == 0 else [nothing, basis]
            stacked = jnp.concatenate(pair + pair, axis=0)
            outer[pl.ds(part * rows // 2, rows // 2)] = jnp.dot(
                both, stacked, preferred_element_type=jnp.float32
            ).reshape(rows // 2, matrices, width)

    for chunk in range(total):
        stage_core(chunk)
        if chunk >= 1:
            stage_x(chunk - 1)
    stage_x(total - 1)
    project()
    for tick in range(total + 3):
        if tick < total:
            stage_z(tick)
        if tick == 1:
            expand()
        if 0 <= tick - 1 < total:
            stage_y(tick - 1)
        if 0 <= tick - 2 < total:
            stage_relay(tick - 2)
        if 0 <= tick - 3 < total:
            stage_end(tick - 3)
    for chunk in range(total):
        core_copy(chunk).wait_send()
        for step in range(1, WIDE):
            x_copy(chunk, step).wait_send()
        for step in range(1, DEPTH):
            z_copy(chunk, step).wait_send()
        to_right(chunk).wait_send()
        to_left(chunk).wait_send()
        onward(chunk).wait_send()


def routed(caps, number, table, moment, deltas, basis_t, theta):
    chip_cap, row_cap = caps
    slots, _, _, _, piece, tiles, lanes = moment.shape
    matrices = theta.shape[1]
    half = deltas.shape[0] // 2
    chunks = len(CHUNKS)
    anywhere = pl.BlockSpec(memory_space=pl.ANY)
    vmem = pl.BlockSpec(memory_space=pltpu.VMEM)

    def buffers(dtype, *lead):
        return [pltpu.VMEM(lead + (n, tiles, lanes), dtype) for _, n in CHUNKS]

    def pair(*shape):
        return [pltpu.SemaphoreType.DMA(shape), pltpu.SemaphoreType.DMA(shape)]

    return pl.pallas_call(
        functools.partial(route, chip_cap, row_cap),
        name="route_%d_%d" % caps,
        out_shape=jax.ShapeDtypeStruct(theta.shape, jnp.bfloat16),
        in_specs=[pl.BlockSpec(memory_space=pltpu.SMEM), anywhere, anywhere, vmem, anywhere],
        out_specs=vmem,
        scratch_shapes=[
            buffers(jnp.float32, slots, DEPTH, WIDE, CORES),
            buffers(jnp.bfloat16, slots, WIDE, DEPTH),
            buffers(jnp.bfloat16, CORES * slots, WIDE, DEPTH),
            buffers(jnp.bfloat16, WIDE, chip_cap, DEPTH),
            buffers(jnp.bfloat16, WIDE * chip_cap, DEPTH),
            buffers(jnp.bfloat16, DEPTH, row_cap),
            buffers(jnp.bfloat16, DEPTH * row_cap),
            pltpu.VMEM((REPS, piece, matrices // 8, tiles, 8, lanes), jnp.bfloat16),
            pltpu.VMEM((REPS, half, 2 * basis_t.shape[0]), jnp.bfloat16),
            pltpu.VMEM(deltas.shape, jnp.bfloat16),
            pltpu.VMEM(theta.shape, jnp.bfloat16),
            pltpu.VMEM(theta.shape, jnp.float32),
            pltpu.SemaphoreType.DMA((chunks + 2,)),
            *pair(chunks),
            *pair(chunks, WIDE - 1),
            *pair(chunks, DEPTH - 1),
            *pair(chunks, 3),
            *pair(3),
        ],
        compiler_params=pltpu.CompilerParams(
            collective_id=number, has_side_effects=True, vmem_limit_bytes=56 << 20
        ),
    )(table, moment, deltas, basis_t, theta)


def per_device(theta, deltas, momentum, basis, slot_matrix):
    matrices, rows, width = theta.shape
    slots, dev_count = momentum.shape[0], momentum.shape[1]
    piece = momentum.shape[3]
    entries = slots * dev_count
    per_chip = slots * CORES
    per_row = per_chip * WIDE

    moment = momentum.reshape(slots, DEPTH, WIDE, CORES, piece, width // 128, 128)
    by_row = deltas[0].transpose(1, 0, 2).reshape(rows * matrices, width)

    dev = lax.axis_index("dev")
    place = jnp.arange(entries, dtype=jnp.int32)
    chip, row = place // per_chip, place // per_row
    filled = slot_matrix >= 0
    before = filled[None, :] & (place[None, :] < place[:, None])
    in_chip = jnp.sum((before & (chip[None, :] == chip[:, None])).astype(jnp.int32), axis=1)
    in_row = jnp.sum((before & (row[None, :] == row[:, None])).astype(jnp.int32), axis=1)
    line = jnp.arange(per_chip + per_row + matrices, dtype=jnp.int32)[:, None]
    of_chip, of_row = line < per_chip, line < per_chip + per_row
    chosen = jnp.where(
        of_chip,
        filled & (chip == dev // CORES) & (in_chip == line),
        jnp.where(
            of_row,
            filled & (row == dev // (CORES * WIDE)) & (in_row == line - per_chip),
            slot_matrix == line - per_chip - per_row,
        ),
    )
    value = jnp.where(
        of_chip, place % per_chip, jnp.where(of_row, chip % WIDE * per_chip + in_chip, row * per_row + in_row)
    )
    table = jnp.sum(jnp.where(chosen, value, 0), axis=1)
    most_chip = jnp.max(jnp.where(filled, in_chip, 0)) + 1
    most_row = jnp.max(jnp.where(filled, in_row, 0)) + 1
    which = sum(((most_chip > a) | (most_row > b)).astype(jnp.int32) for a, b in CAPS[:-1])

    def branch(number):
        return lambda: routed(
            CAPS[number], number, table, moment, by_row, basis.T, theta.transpose(1, 0, 2)
        )

    return lax.switch(which, [branch(n) for n in range(len(CAPS))]).transpose(1, 0, 2)


def solution(mesh):
    placed = (
        P(None, "dev", None),
        P("rep", None, "dev", None),
        P("dev", None, "rep", None, None),
        P(),
        P(),
    )
    return jax.shard_map(
        per_device, mesh=mesh, in_specs=placed, out_specs=P(None, "dev", None), check_vma=False,
    )
```

time: 183 us -> 64.8 us (0.35)
  waiting for transfers between devices: 72.5 us -> 0 us
  Pallas kernels: 0 us -> 57.5 us
  local copies, waits for them, and re-layouts: 36 us -> 1.34 us
  other arithmetic: 27.5 us -> 3.09 us
  blocking collectives: 14.5 us -> 0 us
  starting transfers between devices: 13.2 us -> 0 us
  between operations: 13.5 us -> 1.39 us
  matrix products: 5.22 us -> 0 us
    all_to_all x1 -> x0, waiting for transfers between devices: 66.5 us -> none  [per_device(): lax.all_to_all(moment, 'dev', split_axis=1, concat_axis=1, tiled=True)]
    pallas_call x0 -> x1, Pallas kernels: none -> 57.5 us  [routed(): pl.pallas_call(functools.partial(route, chip_cap, row_cap), name='route_%...]
    convert_element_type x3 -> x0, other arithmetic: 24.3 us -> none  [the longest x1 18.4 us: per_device(): momentum.reshape(slots, dev_count, piece * width).astype(jnp.bfloat16)]
    all_gather x1 -> x0, blocking collectives: 14.5 us -> none  [per_device(): every = lax.all_gather(compressed, 'rep', axis=0, tiled=False)]
    all_to_all x1 -> x0, starting transfers between devices: 13.2 us -> none  [per_device(): lax.all_to_all(moment, 'dev', split_axis=1, concat_axis=1, tiled=True)]
    convert_element_type x3 -> x0, local copies, waits for them, and re-layouts: 11.9 us -> none  [the longest x2 9.38 us: per_device(): momentum.reshape(slots, dev_count, piece * width).astype(jnp.bfloat16)]
    mul x2 -> x0, local copies, waits for them, and re-layouts: 11.1 us -> none  [per_device(): renewed = momentum_rate * moments + outer]
    all_gather x1 -> x0, waiting for transfers between devices: 6.06 us -> none  [per_device(): lax.all_gather(chosen.reshape(matrices, 1, piece * width), 'rep', axis=1,...]
  transfers between devices with their start and end apart: 2 -> 0, of which waited for: 2 -> 0; matrix products, arithmetic and copies ran while one was open for 8% -> 0% of each run, Pallas kernels for 0% -> 0%
where the time goes in v3:
time: 64.8 us; the launch traced here: 63.7 us
  Pallas kernels  57.5 us (89%)
  other arithmetic  3.09 us (5%)
  between operations  1.39 us (2%)
  local copies, waits for them, and re-layouts  1.34 us (2%)
    pallas_call x1, Pallas kernels, routed(): pl.pallas_call(functools.partial(route, chip_cap, row_cap), name='route_%...  57.5 us
    reduce_max x1, other arithmetic, per_device(): most_row = jnp.max(jnp.where(filled, in_row, 0)) + 1  1.38 us
    unnamed x1, local copies, waits for them, and re-layouts  1.34 us

profile of v3, /device:TPU:1, one launch (start us, length us, event | category | flops | bytes accessed | tf_op | source)
XLA Modules:
  0.0 63.7 jit_solution(16986753315299491993)
XLA Ops:
  0.0 0.7 %compare_and_fusion.1 = (pred[128]{0:T(512)(128)(4,1)S(1)}, pred[128]{0:T(512)(128)(4,1)S(1)}, pred[128]{0:T(512)(128)(4,1)S(1)}) fusion(s32[]{:T(128)S(6)} %select_n.80, s32[128]{0:T(128)} %param.12, s32[]{:T(128)S(6)} %select_n.81), kind=kLoop, calls=%fused_computation.15 | loop fusion | flops 2432 | bytes 904 | tf_op jit(solution)/shard_map/and | solution.py:313
  0.7 0.2 convert_reduce_fusion
  0.9 1.4 %select_reduce_fusion.1 = (s32[]{:T(128)}, s32[]{:T(128)}, s32[128]{0:T(128)S(1)}, s32[128]{0:T(128)S(1)}) fusion(s32[128]{0:T(128)S(1)} %get-tuple-element.56, s32[128]{0:T(128)} %param.12, s32[128]{0:T(128)S(1)} %get-tuple-element.57), kind=kLoop, calls=%fused_computation.31 | loop fusion | flops 4350 | bytes 2568 | tf_op jit(solution)/shard_map/reduce_max | solution.py:325
  3.6 0.9 %select_reduce_fusion = s32[44]{0:T(128)S(1)} fusion(s32[128]{0:T(128)S(1)} %get-tuple-element.62, s32[128]{0:T(128)S(1)} %get-tuple-element.61, s32[128]{0:T(128)S(1)} %and_select_fusion.1, s32[128]{0:T(128)} %param.12, s32[128]{0:T(128)S(1)} %get-tuple-element.56, s32[128]{0:T(128)S(1)} %get-tuple-element.57, s32[44]{0:T(128)S(1)} %get-tuple-element.65, ...), kind=kLoop, calls=%fused_computation.6 | loop fusion | flops 61908 | bytes 3944 | tf_op jit(solution)/shard_map/reduce_sum | solution.py:323
  4.5 57.8 %conditional.1 = (bf16[44,24,1024]{2,1,0:T(8,128)(2,1)S(1)}) conditional(s32[]{:T(128)} %clamp.3, (bf16[1024,64]{0,1:T(8,128)(2,1)}, bf16[24,44,1024]{2,0,1:T(8,128)(2,1)}, s32[44]{0:T(128)S(1)}, f32[2,8,4,2,11,8,128]{6,5,4,3,2,1,0:T(8,128)}, bf16[1056,1024]{1,0:T(8,128)(2,1)}) %tuple.30, (bf16[1024,64]{0,1:T(8,128)(2,1)}, ...), branch_computations={%region_5.6_spmd, %region_6.7_spmd, %region_7.8_spmd} | conditional | bytes 8 | solution.py:333
  4.5 57.5 %route_3_6.1 = bf16[44,24,1024]{2,1,0:T(8,128)(2,1)S(1)} custom-call(s32[44]{0:T(128)S(1)} %get-tuple-element.38.table_ref, f32[2,8,4,2,11,8,128]{6,5,4,3,2,1,0:T(8,128)} %get-tuple-element.40.mom_ref, bf16[1056,1024]{1,0:T(8,128)(2,1)} %get-tuple-element.41.deltas_ref, bf16[64,1024]{1,0:T(8,128)(2,1)} %bitcast.23, bf16[44,24,1024]{2,1,0:T(8,128)(2,1)} %bitcast.16), custom_call_target="tpu_custom_call" | custom-call | tf_op jit(solution)/shard_map/cond/branch_0_fun/route_3_6/pallas_call | solution.py:259
  62.3 1.3 %copy.10 = bf16[24,44,1024]{2,0,1:T(8,128)(2,1)} copy(bf16[24,44,1024]{2,0,1:T(8,128)(2,1)S(1)} %bitcast.22) | data formatting | bytes 4325376
  (4 shorter events, 0.0 us)

commit v4 on v3

--- a/solution.py
+++ b/solution.py
@@ -14,8 +14,11 @@
 WIDE = 4
 DEPTH = 8
 REPS = 4
-CHUNKS = ((0, 3), (3, 3), (6, 3), (9, 2))
-CAPS = ((3, 6), (4, 8), (4, 16))
+CHUNKS = ((0, 2), (2, 2), (4, 2), (6, 2), (8, 2), (10, 1))
+CAPS = ((2, 5), (3, 6), (4, 8), (4, 16))
+WINDOW = 2
+X_STEPS = (2, 1, 3)
+Z_STEPS = (4, 3, 5, 2, 6, 1, 7)
 
 
 def route(
@@ -121,7 +124,7 @@
         core_copy(chunk).wait_recv()
         for slot in range(chip_cap):
             x_out[chunk][:, slot] = chip_in[chunk][table_ref[slot]]
-        for step in range(1, WIDE):
+        for step in X_STEPS:
             x_copy(chunk, step).start()
         row_in[chunk][pl.ds(x * chip_cap, chip_cap)] = x_out[chunk][x]
 
@@ -131,7 +134,7 @@
         for slot in range(row_cap):
             code = table_ref[4 + slot]
             z_out[chunk][:, slot] = row_in[chunk][code // 4 * chip_cap + lax.rem(code, 4)]
-        for step in range(1, DEPTH):
+        for step in Z_STEPS:
             z_copy(chunk, step).start()
         z_in[chunk][pl.ds(z * row_cap, row_cap)] = z_out[chunk][z]
 
@@ -215,13 +218,16 @@
 
     for chunk in range(total):
         stage_core(chunk)
-        if chunk >= 1:
+        if 1 <= chunk <= WINDOW:
             stage_x(chunk - 1)
-    stage_x(total - 1)
+    if WINDOW == total:
+        stage_x(total - 1)
     project()
     for tick in range(total + 3):
         if tick < total:
             stage_z(tick)
+            if tick + WINDOW < total:
+                stage_x(tick + WINDOW)
         if tick == 1:
             expand()
         if 0 <= tick - 1 < total:

time: 64.8 us -> 61.6 us (0.951)
  Pallas kernels: 57.5 us -> 54.3 us
    pallas_call x1, Pallas kernels: 57.5 us -> 54.3 us  [routed(): pl.pallas_call(functools.partial(route, chip_cap, row_cap), name='route_%...]
where the time goes in v4:
time: 61.6 us; the launch traced here: 60.8 us
  Pallas kernels  54.3 us (88%)
  other arithmetic  3.09 us (5%)
  between operations  1.4 us (2%)
  local copies, waits for them, and re-layouts  1.34 us (2%)
  loops' own time  0.74 us (1%)
    pallas_call x1, Pallas kernels, routed(): pl.pallas_call(functools.partial(route, chip_cap, row_cap), name='route_%...  54.3 us
    reduce_max x1, other arithmetic, per_device(): most_row = jnp.max(jnp.where(filled, in_row, 0)) + 1  1.38 us
    unnamed x1, local copies, waits for them, and re-layouts  1.34 us

profile of v4, /device:TPU:1, one launch (start us, length us, event | category | flops | bytes accessed | tf_op | source)
XLA Modules:
  0.0 60.8 jit_solution(18204441462770418181)
XLA Ops:
  0.0 0.7 %compare_and_fusion.1 = (pred[128]{0:T(512)(128)(4,1)S(1)}, pred[128]{0:T(512)(128)(4,1)S(1)}, pred[128]{0:T(512)(128)(4,1)S(1)}) fusion(s32[]{:T(128)S(6)} %select_n.80, s32[128]{0:T(128)} %param.13, s32[]{:T(128)S(6)} %select_n.81), kind=kLoop, calls=%fused_computation.15 | loop fusion | flops 2432 | bytes 904 | tf_op jit(solution)/shard_map/and | solution.py:319
  0.7 0.2 convert_reduce_fusion
  0.9 1.4 %select_reduce_fusion.1 = (s32[]{:T(128)}, s32[]{:T(128)}, s32[128]{0:T(128)S(1)}, s32[128]{0:T(128)S(1)}) fusion(s32[128]{0:T(128)S(1)} %get-tuple-element.72, s32[128]{0:T(128)} %param.13, s32[128]{0:T(128)S(1)} %get-tuple-element.73), kind=kLoop, calls=%fused_computation.31 | loop fusion | flops 4350 | bytes 2568 | tf_op jit(solution)/shard_map/reduce_max | solution.py:331
  3.6 0.9 %select_reduce_fusion = s32[44]{0:T(128)S(1)} fusion(s32[128]{0:T(128)S(1)} %get-tuple-element.78, s32[128]{0:T(128)S(1)} %get-tuple-element.77, s32[128]{0:T(128)S(1)} %and_select_fusion.1, s32[128]{0:T(128)} %param.13, s32[128]{0:T(128)S(1)} %get-tuple-element.72, s32[128]{0:T(128)S(1)} %get-tuple-element.73, s32[44]{0:T(128)S(1)} %get-tuple-element.81, ...), kind=kLoop, calls=%fused_computation.6 | loop fusion | flops 61908 | bytes 3944 | tf_op jit(solution)/shard_map/reduce_sum | solution.py:329
  4.5 55.0 %conditional.1 = (bf16[44,24,1024]{2,1,0:T(8,128)(2,1)S(1)}) conditional(s32[]{:T(128)} %clamp.3, (bf16[1024,64]{0,1:T(8,128)(2,1)}, bf16[24,44,1024]{2,0,1:T(8,128)(2,1)}, s32[44]{0:T(128)S(1)}, f32[2,8,4,2,11,8,128]{6,5,4,3,2,1,0:T(8,128)}, bf16[1056,1024]{1,0:T(8,128)(2,1)}) %tuple.35, ...), branch_computations={%region_5.6_spmd, %region_6.7_spmd, %region_7.8_spmd, %region_8.9_... | conditional | bytes 8 | solution.py:339
  4.7 54.3 %route_3_6.1 = bf16[44,24,1024]{2,1,0:T(8,128)(2,1)S(1)} custom-call(s32[44]{0:T(128)S(1)} %get-tuple-element.55.table_ref, f32[2,8,4,2,11,8,128]{6,5,4,3,2,1,0:T(8,128)} %get-tuple-element.56.mom_ref, bf16[1056,1024]{1,0:T(8,128)(2,1)} %get-tuple-element.57.deltas_ref, bf16[64,1024]{1,0:T(8,128)(2,1)} %bitcast.29, bf16[44,24,1024]{2,1,0:T(8,128)(2,1)} %bitcast.20), custom_call_target="tpu_custom_call" | custom-call | tf_op jit(solution)/shard_map/cond/branch_1_fun/route_3_6/pallas_call | solution.py:265
  59.5 1.3 %copy.11 = bf16[24,44,1024]{2,0,1:T(8,128)(2,1)} copy(bf16[24,44,1024]{2,0,1:T(8,128)(2,1)S(1)} %bitcast.27) | data formatting | bytes 4325376
  (4 shorter events, 0.0 us)

commit v5 on v4

--- a/solution.py
+++ b/solution.py
@@ -14,7 +14,7 @@
 WIDE = 4
 DEPTH = 8
 REPS = 4
-CHUNKS = ((0, 2), (2, 2), (4, 2), (6, 2), (8, 2), (10, 1))
+CHUNKS = ((0, 1), (1, 2), (3, 2), (5, 2), (7, 2), (9, 2))
 CAPS = ((2, 5), (3, 6), (4, 8), (4, 16))
 WINDOW = 2
 X_STEPS = (2, 1, 3)
@@ -123,7 +123,7 @@
     def stage_x(chunk):
         core_copy(chunk).wait_recv()
         for slot in range(chip_cap):
-            x_out[chunk][:, slot] = chip_in[chunk][table_ref[slot]]
+            x_out[chunk][:, slot] = chip_in[chunk][table_ref[0, slot]]
         for step in X_STEPS:
             x_copy(chunk, step).start()
         row_in[chunk][pl.ds(x * chip_cap, chip_cap)] = x_out[chunk][x]
@@ -132,7 +132,7 @@
         for step in range(1, WIDE):
             x_copy(chunk, step).wait_recv()
         for slot in range(row_cap):
-            code = table_ref[4 + slot]
+            code = table_ref[0, 4 + slot]
             z_out[chunk][:, slot] = row_in[chunk][code // 4 * chip_cap + lax.rem(code, 4)]
         for step in Z_STEPS:
             z_copy(chunk, step).start()
@@ -143,7 +143,7 @@
         for step in range(1, DEPTH):
             z_copy(chunk, step).wait_recv()
         for group in range(moments.shape[2]):
-            codes = [table_ref[20 + group * 8 + m] for m in range(8)]
+            codes = [table_ref[0, 20 + group * 8 + m] for m in range(8)]
             picks = [code // 16 * row_cap + lax.rem(code, 16) for code in codes]
             for line in range(count):
                 tile = jnp.stack([z_in[chunk][pick, line].astype(jnp.float32) for pick in picks], axis=0)
@@ -294,6 +294,52 @@
     )(table, moment, deltas, basis_t, theta)
 
 
+def arrange(per_chip, per_row, matrices, slot_ref, table_ref, which_ref):
+    dev = lax.axis_index("dev")
+    entries = slot_ref.shape[1]
+    square = (entries, entries)
+    across = jnp.broadcast_to(slot_ref[...], square)
+    down = across.T
+    place = lax.broadcasted_iota(jnp.int32, square, 0)
+    line = lax.broadcasted_iota(jnp.int32, square, 1)
+    chip, row = place // per_chip, place // per_row
+    before = (across >= 0) & (line < place)
+    in_chip = jnp.sum(jnp.where(before & (line // per_chip == chip), 1, 0), axis=1, keepdims=True)
+    in_row = jnp.sum(jnp.where(before & (line // per_row == row), 1, 0), axis=1, keepdims=True)
+    filled = down >= 0
+    of_chip, of_row = line < per_chip, line < per_chip + per_row
+    in_mine = (chip == dev // CORES) & (in_chip == line)
+    in_line = (row == dev // (CORES * WIDE)) & (in_row == line - per_chip)
+    held = down == line - per_chip - per_row
+    value = jnp.where(
+        of_chip,
+        jnp.where(filled & in_mine, place % per_chip, 0),
+        jnp.where(
+            of_row,
+            jnp.where(filled & in_line, chip % WIDE * per_chip + in_chip, 0),
+            jnp.where(filled & held, row * per_row + in_row, 0),
+        ),
+    )
+    table_ref[...] = jnp.sum(value, axis=0, keepdims=True)
+    needed = jnp.zeros(square, jnp.int32)
+    for chip_cap, row_cap in CAPS[:-1]:
+        needed += jnp.where((in_chip >= chip_cap) | (in_row >= row_cap), 1, 0)
+    which_ref[0, 0] = jnp.max(jnp.where(filled, needed, 0))
+
+
+def planned(slot_row, per_chip, per_row, matrices):
+    return pl.pallas_call(
+        functools.partial(arrange, per_chip, per_row, matrices),
+        name="arrange",
+        out_shape=(
+            jax.ShapeDtypeStruct(slot_row.shape, jnp.int32),
+            jax.ShapeDtypeStruct((1, 1), jnp.int32),
+        ),
+        in_specs=[pl.BlockSpec(memory_space=pltpu.VMEM)],
+        out_specs=(pl.BlockSpec(memory_space=pltpu.VMEM), pl.BlockSpec(memory_space=pltpu.SMEM)),
+    )(slot_row)
+
+
 def per_device(theta, deltas, momentum, basis, slot_matrix):
     matrices, rows, width = theta.shape
     slots, dev_count = momentum.shape[0], momentum.shape[1]
@@ -305,38 +351,14 @@
     moment = momentum.reshape(slots, DEPTH, WIDE, CORES, piece, width // 128, 128)
     by_row = deltas[0].transpose(1, 0, 2).reshape(rows * matrices, width)
 
-    dev = lax.axis_index("dev")
-    place = jnp.arange(entries, dtype=jnp.int32)
-    chip, row = place // per_chip, place // per_row
-    filled = slot_matrix >= 0
-    before = filled[None, :] & (place[None, :] < place[:, None])
-    in_chip = jnp.sum((before & (chip[None, :] == chip[:, None])).astype(jnp.int32), axis=1)
-    in_row = jnp.sum((before & (row[None, :] == row[:, None])).astype(jnp.int32), axis=1)
-    line = jnp.arange(per_chip + per_row + matrices, dtype=jnp.int32)[:, None]
-    of_chip, of_row = line < per_chip, line < per_chip + per_row
-    chosen = jnp.where(
-        of_chip,
-        filled & (chip == dev // CORES) & (in_chip == line),
-        jnp.where(
-            of_row,
-            filled & (row == dev // (CORES * WIDE)) & (in_row == line - per_chip),
-            slot_matrix == line - per_chip - per_row,
-        ),
-    )
-    value = jnp.where(
-        of_chip, place % per_chip, jnp.where(of_row, chip % WIDE * per_chip + in_chip, row * per_row + in_row)
-    )
-    table = jnp.sum(jnp.where(chosen, value, 0), axis=1)
-    most_chip = jnp.max(jnp.where(filled, in_chip, 0)) + 1
-    most_row = jnp.max(jnp.where(filled, in_row, 0)) + 1
-    which = sum(((most_chip > a) | (most_row > b)).astype(jnp.int32) for a, b in CAPS[:-1])
+    table, which = planned(slot_matrix.reshape(1, entries), per_chip, per_row, matrices)
 
     def branch(number):
         return lambda: routed(
             CAPS[number], number, table, moment, by_row, basis.T, theta.transpose(1, 0, 2)
         )
 
-    return lax.switch(which, [branch(n) for n in range(len(CAPS))]).transpose(1, 0, 2)
+    return lax.switch(which.reshape(()), [branch(n) for n in range(len(CAPS))]).transpose(1, 0, 2)
 
 
 def solution(mesh):

time: 61.6 us -> 58.9 us (0.956); the launches traced: 60.8 us -> 58.7 us
  other arithmetic: 3.09 us -> 0 us
  Pallas kernels: 54.3 us -> 56 us
  between operations: 1.4 us -> 0.67 us
    pallas_call x0 -> x1, Pallas kernels: none -> 1.58 us  [planned(): pl.pallas_call(functools.partial(arrange, per_chip, per_row, matrices), n...]
    reduce_max x1 -> x0, other arithmetic: 1.38 us -> none  [per_device(): most_row = jnp.max(jnp.where(filled, in_row, 0)) + 1]
    reduce_sum x2 -> x0, other arithmetic: 1.03 us -> none  [the longest x1 0.85 us: per_device(): table = jnp.sum(jnp.where(chosen, value, 0), axis=1)]
    and x1 -> x0, other arithmetic: 0.66 us -> none  [per_device(): filled & (chip == dev // CORES) & (in_chip == line)]
where the time goes in v5:
time: 58.9 us; the launch traced here: 58.7 us
  Pallas kernels  56 us (95%)
  local copies, waits for them, and re-layouts  1.34 us (2%)
  loops' own time  0.73 us (1%)
  between operations  0.67 us (1%)
    pallas_call x1, Pallas kernels, routed(): pl.pallas_call(functools.partial(route, chip_cap, row_cap), name='route_%...  54.4 us
    pallas_call x1, Pallas kernels, planned(): pl.pallas_call(functools.partial(arrange, per_chip, per_row, matrices), n...  1.58 us
    unnamed x1, local copies, waits for them, and re-layouts  1.34 us

profile of v5, /device:TPU:1, one launch (start us, length us, event | category | flops | bytes accessed | tf_op | source)
XLA Modules:
  0.0 58.7 jit_solution(3222849634070447837)
XLA Ops:
  0.0 1.6 %arrange.1 = (s32[1,128]{1,0:T(1,128)S(1)}, s32[1,1]{1,0:T(1,128)}) custom-call(s32[1,128]{1,0:T(1,128)} %bitcast.34), custom_call_target="tpu_custom_call" | custom-call | tf_op jit(solution)/shard_map/arrange/pallas_call | solution.py:331
  2.2 55.2 %conditional.1 = (bf16[44,24,1024]{2,1,0:T(8,128)(2,1)S(1)}) conditional(s32[]{:T(128)} %bitcast.9, (bf16[1024,64]{0,1:T(8,128)(2,1)}, bf16[24,44,1024]{2,0,1:T(8,128)(2,1)}, s32[1,128]{1,0:T(1,128)S(1)}, f32[2,8,4,2,11,8,128]{6,5,4,3,2,1,0:T(8,128)}, bf16[1056,1024]{1,0:T(8,128)(2,1)}) %tuple.26, ...), branch_computations={%region_0.0_spmd, %region_1.0_spmd, %region_2.0_spmd, %region_3.0_... | conditional | bytes 8 | solution.py:361
  2.4 54.4 %route_3_6.1 = bf16[44,24,1024]{2,1,0:T(8,128)(2,1)S(1)} custom-call(s32[1,128]{1,0:T(1,128)S(1)} %get-tuple-element.55.table_ref, f32[2,8,4,2,11,8,128]{6,5,4,3,2,1,0:T(8,128)} %get-tuple-element.56.mom_ref, bf16[1056,1024]{1,0:T(8,128)(2,1)} %get-tuple-element.57.deltas_ref, bf16[64,1024]{1,0:T(8,128)(2,1)} %bitcast.31, bf16[44,24,1024]{2,1,0:T(8,128)(2,1)} %bitcast.22), custom_call_target="tpu_custom_call" | custom-call | tf_op jit(solution)/shard_map/cond/branch_1_fun/route_3_6/pallas_call | solution.py:265
  57.4 1.3 %copy.11 = bf16[24,44,1024]{2,0,1:T(8,128)(2,1)} copy(bf16[24,44,1024]{2,0,1:T(8,128)(2,1)S(1)} %bitcast.29) | data formatting | bytes 4325376
